TPU v7x, 256 devices: a whole 4x4x8 slice. The times are simulated.
256 devices in a mesh: cls: 16 (over y, x), ori: 16 (over z, core).
Axes of the slice: x: 4, y: 4, z: 8, core: 2. Of those that a mesh axis runs over, the one named last changes fastest.
Arguments:
- images: bfloat16 [1024, 2, 2048], P('ori'), may hold values from -500 to 500
- projections: bfloat16 [16, 2048, 2, 2048], P('cls', 'ori'), may hold values from -1 to 1
- ctf_table: bfloat16 [64, 2048], replicated, may hold values from 0.099609375 to 1
- ctf_index: int32 [1024], P('ori'), may hold values from 0 to 63
- centre: int32 [1024, 2], P('ori'), may hold values from -4 to 4
- ranges: int32 [1024, 4], P('ori'), may hold values from 0 to 15, as said below
- inv_noise: float32 [2048], replicated, may hold values from 0.3 to 3
Outputs:
- data_sums: float32 [16, 2048, 2, 2048], P('cls', 'ori')
- ctf_sums: float32 [16, 2048, 2048], P('cls', 'ori')
- log_evidence: float32 [1024], P('ori')
Inputs may be any that keep to these rules, and one draw needn't show every extreme that they name: Each row lists 4 different ranges. Among the rows of one index of ori (aligned blocks of 64 rows) no range is listed by more than 32 rows, and one range is listed by exactly 32 rows in every block.
All inputs are finite; a program needn't handle non-finite values.
Results may differ from a plain program's by a relative error of at most 0.0065.
Values may be sent and summed in bfloat16 or wider, within the bound.
A program may use at most 128 MiB of HBM per device.

v0:
```python
import math

import jax
import jax.numpy as jnp
from jax import lax
from jax.sharding import PartitionSpec as P

KX = 32
KY = 64
BOX = 256
TRANS = 9


def joined_2(value, axis, join):
    pieces = jax.tree.map(lambda part: lax.all_gather(part, axis), value)
    head = jax.tree.map(lambda part: part[0], pieces)
    tail = jax.tree.map(lambda part: part[1:], pieces)
    running, _ = lax.scan(lambda running, piece: (join(running, piece), None), head, tail)
    return running


def slot_layout(route_rows, ori_count, capacity):
    copy_count = route_rows.shape[0] * route_rows.shape[1]
    target = route_rows.reshape(copy_count)
    onehot = (target[:, None] == jnp.arange(ori_count, dtype=jnp.int32)[None, :]).astype(jnp.int32)
    position = jnp.sum(jnp.cumsum(onehot, axis=0) * onehot, axis=1) - 1
    where_to = target * capacity + position
    owners = jnp.arange(copy_count, dtype=jnp.int32) // route_rows.shape[1]
    source = jnp.zeros((ori_count * capacity,), jnp.int32).at[where_to].set(owners)
    filled = jnp.zeros((ori_count * capacity,), jnp.int32).at[where_to].set(1)
    return (where_to, source, filled)


def combine_parts(left_part, right_part):
    left_peak, left_mass = left_part
    right_peak, right_mass = right_part
    joined = jnp.maximum(left_peak, right_peak)
    return (
        joined,
        left_mass * jnp.exp(left_peak - joined) + right_mass * jnp.exp(right_peak - joined),
    )


def shards(images, projections, ctf_table, ctf_index, centre, ranges, inv_noise):
    ori_count = lax.axis_size("ori")
    part_dev = images.shape[0]
    prune_count = ranges.shape[1]
    coef_count = images.shape[2]
    capacity = 2 * part_dev * prune_count // ori_count
    slot_count = ori_count * capacity
    where_to, source, filled = slot_layout(ranges, ori_count, capacity)
    parcel = images[source] * filled[:, None, None].astype(jnp.bfloat16)
    details_out = jnp.stack(
        [ctf_index[source], centre[source, 0], centre[source, 1], source, filled], axis=1
    )
    arrived, details = (
        lax.all_to_all(
            parcel.reshape(ori_count, capacity, 2, coef_count),
            "ori",
            split_axis=0,
            concat_axis=0,
            tiled=True,
        ),
        lax.all_to_all(
            details_out.reshape(ori_count, capacity, 5),
            "ori",
            split_axis=0,
            concat_axis=0,
            tiled=True,
        ),
    )
    arrived = arrived.reshape(slot_count, 2, coef_count)
    details = details.reshape(slot_count, 5)
    is_live = details[:, 4] > 0
    group_count = ctf_table.shape[0]
    pick_ctf = (details[:, 0][:, None] == jnp.arange(group_count, dtype=jnp.int32)[None, :]).astype(
        jnp.bfloat16
    )
    ctf_curve = jnp.dot(pick_ctf, ctf_table, preferred_element_type=jnp.float32)
    ctf_weight = (inv_noise[None, :] * ctf_curve * ctf_curve).astype(jnp.bfloat16)
    class_plane = projections[0]
    ori_dev = class_plane.shape[0]
    flat_plane = class_plane.reshape(ori_dev, 2 * coef_count)
    wide_plane = class_plane.astype(jnp.float32)
    power_plane = (
        wide_plane[:, 0, :] * wide_plane[:, 0, :] + wide_plane[:, 1, :] * wide_plane[:, 1, :]
    ).astype(jnp.bfloat16)
    energy = 0.5 * jnp.dot(ctf_weight, power_plane.T, preferred_element_type=jnp.float32)
    coef_index = jnp.arange(coef_count, dtype=jnp.int32)
    freq_x = coef_index % KX
    freq_y = coef_index // KX - KY // 2
    trans_index = jnp.arange(TRANS, dtype=jnp.int32)
    step_x = trans_index // 3 - 1
    step_y = trans_index % 3 - 1
    radians = 2.0 * math.pi / BOX
    block_rows = math.gcd(64, slot_count)
    block_total = slot_count // block_rows
    starts = jnp.arange(block_total, dtype=jnp.int32) * block_rows

    def rotate_block(row_start):
        pixels = lax.dynamic_slice_in_dim(arrived, row_start, block_rows).astype(jnp.float32)
        curve_block = lax.dynamic_slice_in_dim(ctf_curve, row_start, block_rows)
        move_x = (
            lax.dynamic_slice_in_dim(details[:, 1], row_start, block_rows)[:, None]
            + step_x[None, :]
        )
        move_y = (
            lax.dynamic_slice_in_dim(details[:, 2], row_start, block_rows)[:, None]
            + step_y[None, :]
        )
        phase_sum = (
            freq_x[None, None, :] * move_x[:, :, None] + freq_y[None, None, :] * move_y[:, :, None]
        )
        angles = phase_sum.astype(jnp.float32) * radians
        cosine = jnp.cos(angles)
        sine_part = jnp.sin(angles)
        factor = (curve_block * inv_noise[None, :])[:, None, :]
        real_part = factor * (pixels[:, None, 0, :] * cosine + pixels[:, None, 1, :] * sine_part)
        imag_part = factor * (pixels[:, None, 1, :] * cosine - pixels[:, None, 0, :] * sine_part)
        rotated = jnp.stack([real_part, imag_part], axis=2).astype(jnp.bfloat16)
        return rotated.reshape(block_rows * TRANS, 2 * coef_count)

    def score_block(row_start):
        rotated = rotate_block(row_start)
        cross_term = jnp.dot(rotated, flat_plane.T, preferred_element_type=jnp.float32).reshape(
            block_rows, TRANS, ori_dev
        )
        return cross_term - lax.dynamic_slice_in_dim(energy, row_start, block_rows)[:, None, :]

    scores = lax.map(score_block, starts).reshape(slot_count, TRANS, ori_dev)
    live_scores = jnp.where(is_live[:, None, None], scores, -1e30)
    slot_peak = jnp.max(live_scores, axis=(1, 2))
    slot_mass = jnp.where(
        is_live, jnp.sum(jnp.exp(live_scores - slot_peak[:, None, None]), axis=(1, 2)), 0.0
    )
    peak_classes, mass_classes = joined_2((slot_peak, slot_mass), "cls", combine_parts)
    back_peak, back_mass = (
        lax.all_to_all(
            peak_classes.reshape(ori_count, capacity),
            "ori",
            split_axis=0,
            concat_axis=0,
            tiled=True,
        ),
        lax.all_to_all(
            mass_classes.reshape(ori_count, capacity),
            "ori",
            split_axis=0,
            concat_axis=0,
            tiled=True,
        ),
    )
    copies_peak = back_peak.reshape(slot_count)[where_to].reshape(part_dev, prune_count)
    copies_mass = back_mass.reshape(slot_count)[where_to].reshape(part_dev, prune_count)
    home_peak = jnp.max(copies_peak, axis=1)
    log_home = home_peak + jnp.log(
        jnp.sum(copies_mass * jnp.exp(copies_peak - home_peak[:, None]), axis=1)
    )
    outgoing = jnp.where(filled > 0, log_home[source], 0.0).reshape(ori_count, capacity)
    slot_log = lax.all_to_all(outgoing, "ori", split_axis=0, concat_axis=0, tiled=True).reshape(
        slot_count
    )
    weight_scale = lax.axis_size("cls") * prune_count * ori_dev

    def accumulate(running, row_start):
        data_acc, ctf_acc = running
        rotated = rotate_block(row_start)
        block_scores = lax.dynamic_slice_in_dim(scores, row_start, block_rows)
        slot_logs = lax.dynamic_slice_in_dim(slot_log, row_start, block_rows)
        live_rows = lax.dynamic_slice_in_dim(is_live, row_start, block_rows)
        weight = weight_scale * jnp.exp(block_scores - slot_logs[:, None, None])
        weight = jnp.where(live_rows[:, None, None], weight, 0.0)
        rounded = weight.astype(jnp.bfloat16).reshape(block_rows * TRANS, ori_dev)
        data_acc = data_acc + lax.dot_general(
            rounded, rotated, (((0,), (0,)), ((), ())), preferred_element_type=jnp.float32
        )
        totals = jnp.sum(weight, axis=1).astype(jnp.bfloat16)
        ctf_block = lax.dynamic_slice_in_dim(ctf_weight, row_start, block_rows)
        ctf_acc = ctf_acc + lax.dot_general(
            totals, ctf_block, (((0,), (0,)), ((), ())), preferred_element_type=jnp.float32
        )
        return ((data_acc, ctf_acc), None)

    initial = (
        jnp.zeros((ori_dev, 2 * coef_count), jnp.float32),
        jnp.zeros((ori_dev, coef_count), jnp.float32),
    )
    (data_acc, ctf_acc), _ = lax.scan(accumulate, initial, starts)
    return (
        data_acc.reshape(1, ori_dev, 2, coef_count),
        ctf_acc.reshape(1, ori_dev, coef_count),
        log_home,
    )


def solution(mesh):
    placed = (
        P("ori", None, None),
        P("cls", "ori", None, None),
        P(),
        P("ori"),
        P("ori", None),
        P("ori", None),
        P(),
    )
    return jax.shard_map(
        shards,
        mesh=mesh,
        in_specs=placed,
        out_specs=(P("cls", "ori", None, None), P("cls", "ori", None), P("ori")),
        check_vma=False,
    )
```

profile of v0, /device:TPU:1, one launch (start us, length us, event | category | flops | bytes accessed | tf_op | source)
XLA Modules:
  0.0 975.9 jit_solution(893287618249587324)
XLA Ops:
  12.8 40.1 %select_select_fusion.1 = (s32[512]{0:T(512)S(1)}, pred[512]{0:T(512)(128)(4,1)S(1)}, pred[512]{0:T(512)(128)(4,1)S(1)}, pred[512]{0:T(512)(128)(4,1)S(1)}, pred...) fusion(s32[]{:T(128)} %bitcast.5, s32[]{:T(128)} %bitcast.6, ...), kind=kLoop, calls=%fused_computation.134 | loop fusion | flops 66048 | bytes 36608 | tf_op jit(solution)/shard_map/gather | solution.py:54
  65.0 10.0 %all-to-all-start = ((s32[16,1,160]{2,1,0:T(1,128)}), s32[16,1,160]{2,1,0:T(1,128)S(1)}, u32[]{:S(2)}, u32[]{:S(2)}) async-start(s32[16,1,160]{2,1,0:T(1,128)} %reshape.670), calls=%async_computation | async-start | bytes 32768 | tf_op jit(solution)/shard_map/all_to_all | solution.py:64
  75.0 18.5 %gather_fusion.2 = bf16[512,2,2048]{2,1,0:T(2,128)(2,1)} fusion(bf16[64,2,2048]{2,1,0:T(2,128)(2,1)S(1)} %copy-done, s32[1024]{0:T(1024)S(1)} %pad_clamp_fusion.1), kind=kCustom, calls=%fused_computation.2 | custom fusion | bytes 8390656 | tf_op jit(solution)/shard_map/gather | solution.py:52
  124.0 81.5 %all-to-all-done.1 = bf16[16,32,2,2048]{3,1,2,0:T(8,128)(2,1)} async-done(((bf16[16,32,2,2048]{3,1,2,0:T(8,128)(2,1)}), bf16[16,32,2,2048]{3,1,2,0:T(8,128)(2,1)}, u32[]{:S(2)}, u32[]{:S(2)}) %all-to-all-start.1) | async-done | bytes 4194336 | tf_op jit(solution)/shard_map/all_to_all | solution.py:57
  210.2 219.5 %while.37 = (s32[]{:T(128)}, f32[8,64,9,128]{3,1,2,0:T(8,128)S(1)}, s32[8]{0:T(128)S(1)}, f32[512,2048]{1,0:T(8,128)}, f32[2048]{0:T(1024)S(1)}, /*index=5*/bf16...) while((s32[]{:T(128)}, f32[8,64,9,128]{3,1,2,0:T(8,128)S(1)}, ...), condition=%wide.region_6.7_spmd.clone, body=%wide.region_5.6_spmd.clone.sunk | while | flops 624528640 | bytes 40299360 | solution.py:130
  215.4 19.1 %multiply_convert_fusion.6 = (bf16[64,9,1,2048]{3,0,2,1:T(8,128)(2,1)S(1)}, bf16[64,9,1,2048]{3,0,2,1:T(8,128)(2,1)S(1)}) fusion(f32[64,2048]{1,0:T(8,128)S(1)} %get-tuple-element.752, s32[64,9]{0,1:T(8,128)S(1)} %broadcast_add_fusion.9, s32[2048]{0:T(1024)S(1)} %get-tuple-element.757, s32[64,9]{0,1:T(8,128)S(1)} %broadcast_add_fusion.10, ...), kind=kLoop, calls=%fused_computation.20.clone.1 | loop fusion | flops 17694720 | bytes 6312448 | tf_op jit(solution)/shard_map/convert
  242.9 19.1 %multiply_convert_fusion.6 = (bf16[64,9,1,2048]{3,0,2,1:T(8,128)(2,1)S(1)}, bf16[64,9,1,2048]{3,0,2,1:T(8,128)(2,1)S(1)}) fusion(f32[64,2048]{1,0:T(8,128)S(1)} %get-tuple-element.752, s32[64,9]{0,1:T(8,128)S(1)} %broadcast_add_fusion.9, s32[2048]{0:T(1024)S(1)} %get-tuple-element.757, s32[64,9]{0,1:T(8,128)S(1)} %broadcast_add_fusion.10, ...), kind=kLoop, calls=%fused_computation.20.clone.1 | loop fusion | flops 17694720 | bytes 6312448 | tf_op jit(solution)/shard_map/convert
  270.3 19.1 %multiply_convert_fusion.6 = (bf16[64,9,1,2048]{3,0,2,1:T(8,128)(2,1)S(1)}, bf16[64,9,1,2048]{3,0,2,1:T(8,128)(2,1)S(1)}) fusion(f32[64,2048]{1,0:T(8,128)S(1)} %get-tuple-element.752, s32[64,9]{0,1:T(8,128)S(1)} %broadcast_add_fusion.9, s32[2048]{0:T(1024)S(1)} %get-tuple-element.757, s32[64,9]{0,1:T(8,128)S(1)} %broadcast_add_fusion.10, ...), kind=kLoop, calls=%fused_computation.20.clone.1 | loop fusion | flops 17694720 | bytes 6312448 | tf_op jit(solution)/shard_map/convert
  297.8 19.1 %multiply_convert_fusion.6 = (bf16[64,9,1,2048]{3,0,2,1:T(8,128)(2,1)S(1)}, bf16[64,9,1,2048]{3,0,2,1:T(8,128)(2,1)S(1)}) fusion(f32[64,2048]{1,0:T(8,128)S(1)} %get-tuple-element.752, s32[64,9]{0,1:T(8,128)S(1)} %broadcast_add_fusion.9, s32[2048]{0:T(1024)S(1)} %get-tuple-element.757, s32[64,9]{0,1:T(8,128)S(1)} %broadcast_add_fusion.10, ...), kind=kLoop, calls=%fused_computation.20.clone.1 | loop fusion | flops 17694720 | bytes 6312448 | tf_op jit(solution)/shard_map/convert
  325.2 19.1 %multiply_convert_fusion.6 = (bf16[64,9,1,2048]{3,0,2,1:T(8,128)(2,1)S(1)}, bf16[64,9,1,2048]{3,0,2,1:T(8,128)(2,1)S(1)}) fusion(f32[64,2048]{1,0:T(8,128)S(1)} %get-tuple-element.752, s32[64,9]{0,1:T(8,128)S(1)} %broadcast_add_fusion.9, s32[2048]{0:T(1024)S(1)} %get-tuple-element.757, s32[64,9]{0,1:T(8,128)S(1)} %broadcast_add_fusion.10, ...), kind=kLoop, calls=%fused_computation.20.clone.1 | loop fusion | flops 17694720 | bytes 6312448 | tf_op jit(solution)/shard_map/convert
  352.7 19.1 %multiply_convert_fusion.6 = (bf16[64,9,1,2048]{3,0,2,1:T(8,128)(2,1)S(1)}, bf16[64,9,1,2048]{3,0,2,1:T(8,128)(2,1)S(1)}) fusion(f32[64,2048]{1,0:T(8,128)S(1)} %get-tuple-element.752, s32[64,9]{0,1:T(8,128)S(1)} %broadcast_add_fusion.9, s32[2048]{0:T(1024)S(1)} %get-tuple-element.757, s32[64,9]{0,1:T(8,128)S(1)} %broadcast_add_fusion.10, ...), kind=kLoop, calls=%fused_computation.20.clone.1 | loop fusion | flops 17694720 | bytes 6312448 | tf_op jit(solution)/shard_map/convert
  380.1 19.1 %multiply_convert_fusion.6 = (bf16[64,9,1,2048]{3,0,2,1:T(8,128)(2,1)S(1)}, bf16[64,9,1,2048]{3,0,2,1:T(8,128)(2,1)S(1)}) fusion(f32[64,2048]{1,0:T(8,128)S(1)} %get-tuple-element.752, s32[64,9]{0,1:T(8,128)S(1)} %broadcast_add_fusion.9, s32[2048]{0:T(1024)S(1)} %get-tuple-element.757, s32[64,9]{0,1:T(8,128)S(1)} %broadcast_add_fusion.10, ...), kind=kLoop, calls=%fused_computation.20.clone.1 | loop fusion | flops 17694720 | bytes 6312448 | tf_op jit(solution)/shard_map/convert
  407.5 19.1 %multiply_convert_fusion.6 = (bf16[64,9,1,2048]{3,0,2,1:T(8,128)(2,1)S(1)}, bf16[64,9,1,2048]{3,0,2,1:T(8,128)(2,1)S(1)}) fusion(f32[64,2048]{1,0:T(8,128)S(1)} %get-tuple-element.752, s32[64,9]{0,1:T(8,128)S(1)} %broadcast_add_fusion.9, s32[2048]{0:T(1024)S(1)} %get-tuple-element.757, s32[64,9]{0,1:T(8,128)S(1)} %broadcast_add_fusion.10, ...), kind=kLoop, calls=%fused_computation.20.clone.1 | loop fusion | flops 17694720 | bytes 6312448 | tf_op jit(solution)/shard_map/convert
  430.8 18.1 %all-gather.1 = f32[16,1,512]{2,1,0:T(1,128)S(1)} all-gather(f32[1,1,512]{2,1,0:T(1,128)S(1)} %fusion.58), channel_id=1, replica_groups=mesh['cls'=16,'ori'=16] {'cls'}, dimensions={0}, use_global_device_ids=true | all-gather | bytes 34816 | tf_op jit(solution)/shard_map/all_gather | solution.py:15
  449.0 17.5 %all-gather = f32[16,1,512]{2,1,0:T(1,128)S(1)} all-gather(f32[1,1,512]{2,1,0:T(1,128)S(1)} %reshape.627), channel_id=1, replica_groups=mesh['cls'=16,'ori'=16] {'cls'}, dimensions={0}, use_global_device_ids=true | all-gather | bytes 34816 | tf_op jit(solution)/shard_map/all_gather | solution.py:15
  468.0 16.2 %all-to-all-start.3 = ((f32[16,1,32]{2,1,0:T(1,128)}), f32[16,1,32]{2,1,0:T(1,128)S(1)}, u32[]{:S(2)}, u32[]{:S(2)}) async-start(f32[16,1,32]{2,1,0:T(1,128)} %all_to_all.28), calls=%async_computation.3 | async-start | bytes 16384 | tf_op jit(solution)/shard_map/all_to_all | solution.py:145
  508.0 40.1 %select_select_fusion = f32[512]{0:T(512)S(1)} fusion(pred[512]{0:T(512)(128)(4,1)S(1)} %get-tuple-element.409, pred[512]{0:T(512)(128)(4,1)S(1)} %get-tuple-element.408, pred[512]{0:T(512)(128)(4,1)S(1)} %get-tuple-element.407, pred[512]{0:T(512)(128)(4,1)S(1)} %get-tuple-element.406, pred[512]{0:T(512)(128)(4,1)S(1)} %get-tuple-element.405, ...), kind=kLoop, calls=%fused_computation.133 | loop fusion | flops 33280 | bytes 36608 | tf_op jit(solution)/shard_map/jit(_where)/select_n | solution.py:159
  560.6 412.2 %while.38 = (s32[]{:T(128)}, f32[128,4096]{1,0:T(8,128)S(1)}, f32[128,2048]{1,0:T(8,128)}, s32[8]{0:T(128)S(1)}, pred[512]{0:T(512)(128)(4,1)S(1)}, /*index=5*/f...) while((s32[]{:T(128)}, f32[128,4096]{1,0:T(8,128)S(1)}, ...), condition=%wide.region_15.16_spmd.clone, body=%wide.region_13.15_spmd.clone.sunk | while | flops 659942656 | bytes 51572524 | solution.py:188
  566.0 19.1 %multiply_convert_fusion.7 = (bf16[64,9,1,2048]{3,0,2,1:T(8,128)(2,1)S(1)}, bf16[64,9,1,2048]{3,0,2,1:T(8,128)(2,1)S(1)}) fusion(f32[64,2048]{1,0:T(8,128)S(1)} %get-tuple-element.777, s32[64,9]{0,1:T(8,128)S(1)} %broadcast_add_fusion.11, s32[2048]{0:T(1024)S(1)} %get-tuple-element.782, s32[64,9]{0,1:T(8,128)S(1)} %broadcast_add_fusion.12, ...), kind=kLoop, calls=%fused_computation.60.clone.1 | loop fusion | flops 17694720 | bytes 6312448 | tf_op jit(solution)/shard_map/convert.2
  617.2 19.1 %multiply_convert_fusion.7 = (bf16[64,9,1,2048]{3,0,2,1:T(8,128)(2,1)S(1)}, bf16[64,9,1,2048]{3,0,2,1:T(8,128)(2,1)S(1)}) fusion(f32[64,2048]{1,0:T(8,128)S(1)} %get-tuple-element.777, s32[64,9]{0,1:T(8,128)S(1)} %broadcast_add_fusion.11, s32[2048]{0:T(1024)S(1)} %get-tuple-element.782, s32[64,9]{0,1:T(8,128)S(1)} %broadcast_add_fusion.12, ...), kind=kLoop, calls=%fused_computation.60.clone.1 | loop fusion | flops 17694720 | bytes 6312448 | tf_op jit(solution)/shard_map/convert.2
  638.9 9.3 copy.119
  668.8 19.1 %multiply_convert_fusion.7 = (bf16[64,9,1,2048]{3,0,2,1:T(8,128)(2,1)S(1)}, bf16[64,9,1,2048]{3,0,2,1:T(8,128)(2,1)S(1)}) fusion(f32[64,2048]{1,0:T(8,128)S(1)} %get-tuple-element.777, s32[64,9]{0,1:T(8,128)S(1)} %broadcast_add_fusion.11, s32[2048]{0:T(1024)S(1)} %get-tuple-element.782, s32[64,9]{0,1:T(8,128)S(1)} %broadcast_add_fusion.12, ...), kind=kLoop, calls=%fused_computation.60.clone.1 | loop fusion | flops 17694720 | bytes 6312448 | tf_op jit(solution)/shard_map/convert.2
  690.4 9.3 copy.119
  720.3 19.1 %multiply_convert_fusion.7 = (bf16[64,9,1,2048]{3,0,2,1:T(8,128)(2,1)S(1)}, bf16[64,9,1,2048]{3,0,2,1:T(8,128)(2,1)S(1)}) fusion(f32[64,2048]{1,0:T(8,128)S(1)} %get-tuple-element.777, s32[64,9]{0,1:T(8,128)S(1)} %broadcast_add_fusion.11, s32[2048]{0:T(1024)S(1)} %get-tuple-element.782, s32[64,9]{0,1:T(8,128)S(1)} %broadcast_add_fusion.12, ...), kind=kLoop, calls=%fused_computation.60.clone.1 | loop fusion | flops 17694720 | bytes 6312448 | tf_op jit(solution)/shard_map/convert.2
  742.0 9.3 copy.119
  771.9 19.1 %multiply_convert_fusion.7 = (bf16[64,9,1,2048]{3,0,2,1:T(8,128)(2,1)S(1)}, bf16[64,9,1,2048]{3,0,2,1:T(8,128)(2,1)S(1)}) fusion(f32[64,2048]{1,0:T(8,128)S(1)} %get-tuple-element.777, s32[64,9]{0,1:T(8,128)S(1)} %broadcast_add_fusion.11, s32[2048]{0:T(1024)S(1)} %get-tuple-element.782, s32[64,9]{0,1:T(8,128)S(1)} %broadcast_add_fusion.12, ...), kind=kLoop, calls=%fused_computation.60.clone.1 | loop fusion | flops 17694720 | bytes 6312448 | tf_op jit(solution)/shard_map/convert.2
  823.4 19.1 %multiply_convert_fusion.7 = (bf16[64,9,1,2048]{3,0,2,1:T(8,128)(2,1)S(1)}, bf16[64,9,1,2048]{3,0,2,1:T(8,128)(2,1)S(1)}) fusion(f32[64,2048]{1,0:T(8,128)S(1)} %get-tuple-element.777, s32[64,9]{0,1:T(8,128)S(1)} %broadcast_add_fusion.11, s32[2048]{0:T(1024)S(1)} %get-tuple-element.782, s32[64,9]{0,1:T(8,128)S(1)} %broadcast_add_fusion.12, ...), kind=kLoop, calls=%fused_computation.60.clone.1 | loop fusion | flops 17694720 | bytes 6312448 | tf_op jit(solution)/shard_map/convert.2
  845.1 9.3 copy.119
  875.0 19.1 %multiply_convert_fusion.7 = (bf16[64,9,1,2048]{3,0,2,1:T(8,128)(2,1)S(1)}, bf16[64,9,1,2048]{3,0,2,1:T(8,128)(2,1)S(1)}) fusion(f32[64,2048]{1,0:T(8,128)S(1)} %get-tuple-element.777, s32[64,9]{0,1:T(8,128)S(1)} %broadcast_add_fusion.11, s32[2048]{0:T(1024)S(1)} %get-tuple-element.782, s32[64,9]{0,1:T(8,128)S(1)} %broadcast_add_fusion.12, ...), kind=kLoop, calls=%fused_computation.60.clone.1 | loop fusion | flops 17694720 | bytes 6312448 | tf_op jit(solution)/shard_map/convert.2
  896.7 9.3 copy.119
  926.5 19.1 %multiply_convert_fusion.7 = (bf16[64,9,1,2048]{3,0,2,1:T(8,128)(2,1)S(1)}, bf16[64,9,1,2048]{3,0,2,1:T(8,128)(2,1)S(1)}) fusion(f32[64,2048]{1,0:T(8,128)S(1)} %get-tuple-element.777, s32[64,9]{0,1:T(8,128)S(1)} %broadcast_add_fusion.11, s32[2048]{0:T(1024)S(1)} %get-tuple-element.782, s32[64,9]{0,1:T(8,128)S(1)} %broadcast_add_fusion.12, ...), kind=kLoop, calls=%fused_computation.60.clone.1 | loop fusion | flops 17694720 | bytes 6312448 | tf_op jit(solution)/shard_map/convert.2
  948.2 9.3 copy.119
  (420 shorter events, 338.6 us)
Async XLA Ops:
  0.6 74.4 %copy-start = (bf16[64,2,2048]{2,1,0:T(2,128)(2,1)S(1)}, bf16[64,2,2048]{2,1,0:T(2,128)(2,1)}, u32[]{:S(2)}) copy-start(bf16[64,2,2048]{2,1,0:T(2,128)(2,1)} %param.13) | copy-start | bytes 1572868
  0.6 57.3 %copy-start.2 = (s32[64,2]{0,1:T(2,128)S(1)}, s32[64,2]{0,1:T(2,128)}, u32[]{:S(2)}) copy-start(s32[64,2]{0,1:T(2,128)} %param.17) | copy-start | bytes 1540
  65.0 39.7 %all-to-all-start = ((s32[16,1,160]{2,1,0:T(1,128)}), s32[16,1,160]{2,1,0:T(1,128)S(1)}, u32[]{:S(2)}, u32[]{:S(2)}) async-start(s32[16,1,160]{2,1,0:T(1,128)} %reshape.670), calls=%async_computation | async-start | bytes 32768 | tf_op jit(solution)/shard_map/all_to_all | solution.py:64
  104.8 100.7 %all-to-all-start.1 = ((bf16[16,32,2,2048]{3,1,2,0:T(8,128)(2,1)}), bf16[16,32,2,2048]{3,1,2,0:T(8,128)(2,1)}, u32[]{:S(2)}, u32[]{:S(2)}) async-start(bf16[16,32,2,2048]{3,1,2,0:T(8,128)(2,1)} %copy.99), calls=%async_computation.1 | async-start | bytes 8388608 | tf_op jit(solution)/shard_map/all_to_all | solution.py:57
  111.9 7.2 copy-start.8
  111.9 7.2 copy-start.9
  119.0 4.2 copy-start.5
  121.9 1.4 copy-start.4
  235.0 1.2 copy-start.7
  262.4 1.2 copy-start.7
  289.9 1.2 copy-start.7
  317.3 1.2 copy-start.7
  344.8 1.2 copy-start.7
  372.2 1.2 copy-start.7
  399.7 1.2 copy-start.7
  427.1 1.2 copy-start.7
  429.7 119.2 %copy-start.3 = (f32[8,64,9,128]{3,1,2,0:T(8,128)}, f32[8,64,9,128]{3,1,2,0:T(8,128)S(1)}, u32[]{:S(2)}) copy-start(f32[8,64,9,128]{3,1,2,0:T(8,128)S(1)} %get-tuple-element.181) | copy-start | bytes 7077892
  468.0 23.1 %all-to-all-start.3 = ((f32[16,1,32]{2,1,0:T(1,128)}), f32[16,1,32]{2,1,0:T(1,128)S(1)}, u32[]{:S(2)}, u32[]{:S(2)}) async-start(f32[16,1,32]{2,1,0:T(1,128)} %all_to_all.28), calls=%async_computation.3 | async-start | bytes 16384 | tf_op jit(solution)/shard_map/all_to_all | solution.py:145
  491.1 10.9 %all-to-all-start.2 = ((f32[16,1,32]{2,1,0:T(1,128)}), f32[16,1,32]{2,1,0:T(1,128)S(1)}, u32[]{:S(2)}, u32[]{:S(2)}) async-start(f32[16,1,32]{2,1,0:T(1,128)} %all_to_all.26), calls=%async_computation.2 | async-start | bytes 16384 | tf_op jit(solution)/shard_map/all_to_all | solution.py:138
  505.2 55.4 %copy-start.6 = (f32[64]{0:T(128)}, f32[64]{0:T(128)S(1)}, u32[]{:S(2)}) copy-start(f32[64]{0:T(128)S(1)} %log_add_fusion) | copy-start | bytes 772
  548.9 10.9 %all-to-all-start.4 = ((f32[16,1,32]{2,1,0:T(1,128)}), f32[16,1,32]{2,1,0:T(1,128)S(1)}, u32[]{:S(2)}, u32[]{:S(2)}) async-start(f32[16,1,32]{2,1,0:T(1,128)} %all_to_all.30), calls=%async_computation.4 | async-start | bytes 16384 | tf_op jit(solution)/shard_map/all_to_all | solution.py:160
  972.8 2.8 copy-start.1
where the time goes:
time: 990 us; the launch traced here: 976 us
  other arithmetic  472 us (48%)
  local copies, waits for them, and re-layouts  235 us (24%)
  waiting for transfers between devices  93.2 us (9%)
  matrix products  64.4 us (7%)
  starting transfers between devices  41.1 us (4%)
  blocking collectives  35.6 us (4%)
  loops' own time  32.9 us (3%)
    another operation x18, other arithmetic  306 us
    all_to_all x1, waiting for transfers between devices, shards(): lax.all_to_all(parcel.reshape(ori_count, capacity, 2, coef_count), 'ori',...  81.5 us
    another operation x8, local copies, waits for them, and re-layouts, rotate_block(): rotated = jnp.stack([real_part, imag_part], axis=2).astype(jnp.bfloat16)  74.5 us
    while x24, local copies, waits for them, and re-layouts  63.7 us
    gather x1, other arithmetic, shards(): ctf_index[source]  40.1 us
    select_n x1, other arithmetic, shards(): jnp.where(filled > 0, log_home[source], 0.0).reshape(ori_count, capacity)  40.1 us
    all_gather x2, blocking collectives, joined_2(): pieces = jax.tree.map(lambda part: lax.all_gather(part, axis), value)  35.6 us
    dot_general x8, matrix products, accumulate(): lax.dot_general(rounded, rotated, (((0,), (0,)), ((), ())), preferred_ele...  29.1 us
  transfers between devices with their start and end apart: 5, of which 4 were waited for; matrix products, arithmetic and copies ran while one was open for 5% of the time, Pallas kernels for 0%

commit v1 on v0

v1 whole, which is shorter than its diff:
```python
import functools
import math

import jax
import jax.numpy as jnp
import numpy as np
from jax import lax
from jax.experimental import pallas as pl
from jax.experimental.pallas import tpu as pltpu
from jax.sharding import PartitionSpec as P

KX = 32
KY = 64
BOX = 256
TRANS = 9
N_CLS = 16
N_ORI = 16
SIDE = 4
PART = 64
CAP = 32
SLOTS = N_ORI * CAP
ORI_DEV = 128
COEFS = 2048
GROUPS = 64
CHUNK = COEFS // N_CLS
PRUNE = 4
RADIANS = 2.0 * math.pi / BOX
MESH = pl.DeviceIdType.MESH
F32 = jnp.float32
BF16 = jnp.bfloat16
VMEM_LIMIT = 56 * 1024 * 1024


def step_tables():
    k = np.arange(COEFS)
    kx = k % KX
    ky = k // KX - KY // 2
    cosine = np.zeros((16, COEFS), np.float32)
    sine = np.zeros((16, COEFS), np.float32)
    for a in range(TRANS):
        turn = (kx * (a // 3 - 1) + ky * (a % 3 - 1)) * RADIANS
        cosine[a] = np.cos(turn)
        sine[a] = np.sin(turn)
    return cosine, sine


def wrap(value, size):
    return lax.rem(value + size, size)


def nt_dot(left, right):
    return lax.dot_general(left, right, (((1,), (1,)), ((), ())), preferred_element_type=F32)


def tn_dot(left, right):
    return lax.dot_general(left, right, (((0,), (0,)), ((), ())), preferred_element_type=F32)


def slot_row(rows_ref, n):
    groups = []
    for q in range(4):
        parts = [rows_ref[4 * q + m, n:n + 1, :] for m in range(4)]
        groups.append((parts[0] + parts[1]) + (parts[2] + parts[3]))
    return jnp.concatenate(groups, axis=1)


def iota(shape, axis):
    return lax.broadcasted_iota(jnp.int32, shape, axis)


HALF = SLOTS // 2
COMBOS = 96
PIECE = HALF // 2


def expect_kernel(images_ref, proj_ref, ctf_ref, index_ref, centre_ref, ranges_ref, inv_ref, cos_ref, sin_ref,
                  yout_ref, w_ref, t_ref, cw_ref, log_ref,
                  ximg, pbuf, send, meta, metain, ys, pd, s_ref, joint, shared, maps, yc, hot, trig, buf_a, buf_b,
                  local_sem, z_send, z_recv, m_send, m_recv, f_send, p_send, g_recv, e_send, e_recv):
    c = lax.axis_index("cls")
    h = lax.axis_index("ori")
    x = lax.rem(c, SIDE)
    y = lax.div(c, SIDE)

    def at(dx, dy):
        return wrap(y + dy, SIDE) * SIDE + wrap(x + dx, SIDE)

    def rel(half, du, dv):
        if isinstance(half, int):
            return at(du, dv) if half == 0 else at(dv, du)
        return at(du + half * (dv - du), dv + half * (du - dv))

    barrier = pltpu.get_barrier_semaphore()

    def quad_peer(stage, j):
        if stage == 0:
            return at(j, 0), h
        if stage == 1:
            return at(0, j), h
        if stage == 2:
            return c, lax.div(h, 4) * 4 + lax.rem(h + j, 4)
        return c, lax.rem(h + 4 * j, N_ORI)

    def greet(step, carry):
        pl.semaphore_signal(barrier, inc=1, device_id=(c, wrap(h + step, N_ORI)), device_id_type=MESH)
        return carry

    for stage in (0, 1):
        for j in (1, 2, 3):
            pl.semaphore_signal(barrier, inc=1, device_id=quad_peer(stage, j), device_id_type=MESH)
    lax.fori_loop(1, N_ORI, greet, 0)
    lanes = pl.ds(pl.multiple_of(c * CHUNK, CHUNK), CHUNK)
    get_image = pltpu.make_async_copy(images_ref.at[:, :, lanes], ximg, local_sem.at[0])
    get_image.start()
    get_proj = pltpu.make_async_copy(proj_ref.at[0], pbuf, local_sem.at[1])
    get_proj.start()

    index_row = index_ref[...].astype(F32)
    member_t = jnp.zeros((N_ORI, PART), F32)
    rank = iota((N_ORI, PART), 0)
    for j in range(PRUNE):
        member_t = member_t + (ranges_ref[j:j + 1, :] == rank).astype(F32)
    above = (iota((PART, PART), 0) < iota((PART, PART), 1)).astype(BF16)
    before_t = jnp.dot(member_t.astype(BF16), above, preferred_element_type=F32)
    pos_t = before_t - 1000.0 * (1.0 - member_t)
    odd = lax.rem(h, 2).astype(F32)
    key = (before_t + 1.0) * member_t
    keys = jnp.concatenate([key * (1.0 - odd), key * odd], axis=1)
    seat = iota((CAP, PART), 0).astype(F32)
    chosen = jnp.concatenate(
        [(pos_t[r:r + 1, :] == seat).astype(BF16) for r in range(N_ORI)], axis=0
    )
    offset = (CAP * lax.rem(h, 4)).astype(F32)
    wide_seat = iota((128, PART), 0).astype(F32) - offset
    moves = centre_ref[...].astype(F32)
    combo = (moves[0:1, :] + 4.0) * 9.0 + moves[1:2, :] + 4.0
    label = jnp.concatenate([index_row + 1.0, combo, jnp.zeros((6, PART), F32)], axis=0).astype(BF16)
    for r in range(N_ORI):
        wide = (pos_t[r:r + 1, :] == wide_seat).astype(BF16)
        seated = nt_dot(label, wide)
        meta[r] = jnp.concatenate([seated[0:1, :], keys[r:r + 1, :], seated[1:3, :]], axis=0)
    get_image.wait()
    pixels = ximg[...].astype(F32)
    x0 = pixels[:, 0, :]
    x1 = pixels[:, 1, :]
    centred = jnp.concatenate([x0, x1], axis=1).astype(BF16)
    send[...] = jnp.dot(chosen, centred, preferred_element_type=F32).astype(BF16).reshape(N_ORI, CAP, 2 * CHUNK)

    pl.semaphore_wait(barrier, N_ORI - 1 + 6)

    def block_cols(block):
        return pl.ds(pl.multiple_of(block * 2 * CHUNK, 2 * CHUNK), 2 * CHUNK)

    def seat_rows(block):
        return pl.ds(pl.multiple_of(block * CAP, CAP), CAP)

    def parcel(peer, step):
        return pltpu.make_async_remote_copy(
            src_ref=send.at[peer], dst_ref=ys.at[seat_rows(h), block_cols(c)], send_sem=z_send.at[step],
            recv_sem=z_recv.at[h], device_id=(c, peer), device_id_type=MESH)

    def note(peer, step):
        return pltpu.make_async_remote_copy(
            src_ref=meta.at[peer], dst_ref=metain.at[h], send_sem=m_send.at[step],
            recv_sem=m_recv.at[h], device_id=(c, peer), device_id_type=MESH)

    def send_out(step, carry):
        peer = wrap(h + step, N_ORI)
        note(peer, step).start()
        parcel(peer, step).start()
        return carry

    lax.fori_loop(1, N_ORI, send_out, 0)
    own_rows = pltpu.make_async_copy(send.at[h], ys.at[seat_rows(h), block_cols(c)], local_sem.at[2])
    own_rows.start()
    metain[h] = meta[h]

    get_proj.wait()
    s_ref[0:ORI_DEV, 0:GROUPS] = jnp.zeros((ORI_DEV, GROUPS), F32)

    def turn_chunk(j, carry):
        cols = pl.ds(pl.multiple_of(j * CHUNK, CHUNK), CHUNK)
        both = pbuf[:, :, cols].astype(F32)
        p0 = both[:, 0, :]
        p1 = both[:, 1, :]
        power = (p0 * p0 + p1 * p1).astype(BF16)
        table = ctf_ref[:, cols].astype(F32)
        cw = (inv_ref[:, cols] * table * table).astype(BF16)
        cw_ref[:, cols] = cw
        s_ref[0:ORI_DEV, 0:GROUPS] += nt_dot(power, cw)
        for d in range(TRANS):
            rows = pl.ds(d * ORI_DEV, ORI_DEV)
            cd = cos_ref[d:d + 1, cols]
            sd = sin_ref[d:d + 1, cols]
            turned = (p0 * cd - p1 * sd, p1 * cd + p0 * sd)
            for n in (0, 1):
                coarse = turned[n].astype(BF16)
                pd[j, rows, n * CHUNK:(n + 1) * CHUNK] = coarse
                pd[j, rows, (2 + n) * CHUNK:(3 + n) * CHUNK] = (turned[n] - coarse.astype(F32)).astype(BF16)
        k = j * CHUNK + iota((1, CHUNK), 1)
        kx = lax.rem(k, KX)
        ky = lax.div(k, KX) - KY // 2
        which = iota((COMBOS, 1), 0)
        angles = (kx * (lax.div(which, 9) - 4) + ky * (lax.rem(which, 9) - 4)).astype(F32) * RADIANS
        for n, wave in ((0, jnp.cos(angles)), (1, jnp.sin(angles))):
            coarse = wave.astype(BF16)
            span = slice(n * CHUNK, (n + 1) * CHUNK)
            trig[j, 0:GROUPS, span] = jnp.zeros((GROUPS, CHUNK), BF16)
            trig[j, GROUPS:GROUPS + COMBOS, span] = coarse
            trig[j, GROUPS + COMBOS:256, span] = (wave - coarse.astype(F32)).astype(BF16)
        trig[j, 0:GROUPS, 2 * CHUNK:3 * CHUNK] = ctf_ref[:, cols]
        trig[j, GROUPS:256, 2 * CHUNK:3 * CHUNK] = jnp.zeros((2 * COMBOS, CHUNK), BF16)
        return carry

    lax.fori_loop(0, N_CLS, turn_chunk, 0)

    def arrive(step, carry):
        peer = wrap(h - step, N_ORI)
        pltpu.make_async_remote_copy(
            src_ref=send.at[h], dst_ref=ys.at[seat_rows(peer), block_cols(c)], send_sem=z_send.at[0],
            recv_sem=z_recv.at[peer], device_id=(c, peer), device_id_type=MESH).wait_recv()
        pltpu.make_async_remote_copy(
            src_ref=meta.at[h], dst_ref=metain.at[peer], send_sem=m_send.at[0],
            recv_sem=m_recv.at[peer], device_id=(c, peer), device_id_type=MESH).wait_recv()
        return carry

    own_rows.wait()
    lax.fori_loop(1, N_ORI, arrive, 0)

    def full_view(half, block):
        return ys.at[pl.ds(pl.multiple_of(half * HALF, HALF), HALF), block_cols(block)]

    def piece_view(half, block, piece):
        return ys.at[pl.ds(pl.multiple_of(half * HALF + piece * PIECE, PIECE), PIECE), block_cols(block)]

    def full_copy(half, block, target, slot):
        return pltpu.make_async_remote_copy(
            src_ref=full_view(half, block), dst_ref=full_view(half, block), send_sem=f_send.at[slot],
            recv_sem=g_recv.at[half, block, 0], device_id=(target, h), device_id_type=MESH)

    def piece_copy(half, block, piece, target, slot):
        return pltpu.make_async_remote_copy(
            src_ref=piece_view(half, block, piece), dst_ref=piece_view(half, block, piece),
            send_sem=p_send.at[slot], recv_sem=g_recv.at[half, block, piece],
            device_id=(target, h), device_id_type=MESH)

    def second_sends(half, du, t):
        for n, sign in enumerate((1, -1)):
            full_copy(half, rel(half, du, 0), rel(half, 0, sign), 4 + 4 * t + 2 * half + n).start()

    for half in (0, 1):
        for n, sign in enumerate((1, -1)):
            full_copy(half, rel(half, 0, 0), rel(half, sign, 0), 2 * half + n).start()
    for half in (0, 1):
        second_sends(half, 0, 0)

    row = slot_row(metain, 0) - 1.0
    slot_pick = (iota((GROUPS, SLOTS), 0).astype(F32) == row).astype(BF16)
    combo_pick = (iota((COMBOS, SLOTS), 0).astype(F32) == slot_row(metain, 2)).astype(BF16)
    eye = (iota((256, 256), 0) == iota((256, 256), 1)).astype(BF16)
    hot[...] = tn_dot(jnp.concatenate([slot_pick, combo_pick, combo_pick], axis=0), eye).astype(BF16)
    rest = s_ref[0:ORI_DEV, 0:GROUPS]
    energy = jnp.zeros((ORI_DEV, SLOTS), F32)
    for _ in range(3):
        part = rest.astype(BF16)
        rest = rest - part.astype(F32)
        energy = energy + jnp.dot(part, slot_pick, preferred_element_type=F32)
    less = -0.5 * energy - jnp.where(row < 0.0, 1e30, 0.0)
    for d in range(TRANS):
        s_ref[pl.ds(d * ORI_DEV, ORI_DEV), :] = less

    tall = iota((128, 128), 0).astype(F32)
    side = lax.div(iota((1, 128), 1), PART)
    listed = []
    for p in range(N_ORI // 2):
        keyed = metain[2 * p, 1:2, :] + metain[2 * p + 1, 1:2, :]
        listed.append(keyed)
        target = keyed - 1.0 + (CAP * (2 * (p % 2) + side)).astype(F32)
        target = jnp.where(keyed > 0.0, target, -1000.0)
        maps[p // 2, :, 128 * (p % 2):128 * (p % 2) + 128] = (tall == target).astype(BF16)

    def centre_rows(half, block, buf):
        rows = slice(half * HALF, half * HALF + HALF)
        freqs = pl.ds(pl.multiple_of(block * CHUNK, CHUNK), CHUNK)
        wave = jnp.dot(hot[rows, :], trig[block], preferred_element_type=F32)
        cs = wave[:, 0:CHUNK]
        sn = wave[:, CHUNK:2 * CHUNK]
        factor = wave[:, 2 * CHUNK:3 * CHUNK] * inv_ref[:, freqs]
        raw = ys[rows, block_cols(block)].astype(F32)
        x0 = raw[:, 0:CHUNK]
        x1 = raw[:, CHUNK:2 * CHUNK]
        value = jnp.concatenate([factor * (x0 * cs + x1 * sn), factor * (x1 * cs - x0 * sn)], axis=1)
        coarse = value.astype(BF16)
        buf[:, 0:2 * CHUNK] = coarse
        buf[:, 2 * CHUNK:4 * CHUNK] = (value - coarse.astype(F32)).astype(BF16)
        yc[rows, block_cols(block)] = coarse

    def add_scores(half, block, buf):
        first = pd[block, :, 0:2 * CHUNK]
        second = pd[block, :, 2 * CHUNK:4 * CHUNK]
        coarse = buf[:, 0:2 * CHUNK]
        fine = buf[:, 2 * CHUNK:4 * CHUNK]
        s_ref[:, half * HALF:half * HALF + HALF] += nt_dot(first, coarse) + (
            nt_dot(first, fine) + nt_dot(second, coarse)
        )

    def pair(before, du, dv):
        block = rel(0, du, dv)
        add_scores(1, before, buf_b)
        centre_rows(0, block, buf_a)
        block_b = rel(1, du, dv)
        add_scores(0, block, buf_a)
        centre_rows(1, block_b, buf_b)
        return block_b

    centre_rows(0, c, buf_a)
    add_scores(0, c, buf_a)
    centre_rows(1, c, buf_b)
    before = c
    for t, du, piece, onward in ((1, -1, 0, 1), (2, 1, 1, -1)):
        for half in (0, 1):
            full_copy(half, rel(half, du, 0), c, 0).wait_recv()
            piece_copy(half, rel(half, du, 0), piece, rel(half, onward, 0), 2 * half + piece).start()
        for half in (0, 1):
            second_sends(half, du, t)

    before = lax.fori_loop(0, 2, lambda n, block: pair(block, 2 * n - 1, 0), before)
    for half in (0, 1):
        for piece in (0, 1):
            piece_copy(half, rel(half, 2, 0), piece, c, 0).wait_recv()
        second_sends(half, 2, 3)

    before = pair(before, 2, 0)

    def gray(t):
        return t + lax.div(t, 2) * (1 - 2 * lax.rem(t, 2))

    def cross(t, carry):
        du = gray(t)
        for dv, piece, onward in ((-1, 0, 1), (1, 1, -1)):
            for half in (0, 1):
                full_copy(half, rel(half, du, dv), c, 0).wait_recv()
                piece_copy(half, rel(half, du, dv), piece, rel(half, 0, onward), 4 + 4 * t + 2 * half + piece).start()

        return lax.fori_loop(0, 2, lambda n, block: pair(block, du, 2 * n - 1), carry)

    before = lax.fori_loop(0, 4, cross, before)

    def corner(n, carry):
        du = gray(n)
        for half in (0, 1):
            for piece in (0, 1):
                piece_copy(half, rel(half, du, 2), piece, c, 0).wait_recv()
        return pair(carry, du, 2)

    before = lax.fori_loop(0, 4, corner, before)
    add_scores(1, before, buf_b)
    save = pltpu.make_async_copy(yc, yout_ref, local_sem.at[3])
    save.start()

    peak = s_ref[0:ORI_DEV, :]
    for d in range(1, TRANS):
        peak = jnp.maximum(peak, s_ref[pl.ds(d * ORI_DEV, ORI_DEV), :])
    peak = jnp.max(peak, axis=0, keepdims=True)
    mass = jnp.zeros((ORI_DEV, SLOTS), F32)
    for d in range(TRANS):
        rows = pl.ds(d * ORI_DEV, ORI_DEV)
        value = jnp.exp(s_ref[rows, :] - peak)
        s_ref[rows, :] = value
        mass = mass + value
    total = jnp.sum(mass, axis=0, keepdims=True)
    def split(value):
        parts = []
        for _ in range(3):
            part = value.astype(BF16).astype(F32)
            parts.append(part)
            value = value - part
        return parts

    blank = jnp.zeros((2, 128), F32)
    for q in range(4):
        span = slice(128 * q, 128 * q + 128)
        rows = jnp.concatenate(split(peak[:, span]) + split(total[:, span]) + [blank], axis=0).astype(BF16)
        spread = jnp.dot(rows, maps[q], preferred_element_type=F32)
        particle_peak = spread[0:1, :] + spread[1:2, :] + spread[2:3, :]
        particle_mass = spread[3:4, :] + spread[4:5, :] + spread[5:6, :]
        for n in (0, 1):
            half_span = slice(128 * n, 128 * n + 128)
            p = 2 * q + n
            joint[0, 0, p:p + 1, :] = jnp.where(listed[p] > 0.0, particle_peak[:, half_span], -3e38)
            joint[0, 1, p:p + 1, :] = particle_mass[:, half_span]

    def share(stage, j):
        return pltpu.make_async_remote_copy(
            src_ref=joint.at[stage], dst_ref=shared.at[stage, j - 1], send_sem=e_send.at[stage, j],
            recv_sem=e_recv.at[stage, j], device_id=quad_peer(stage, j), device_id_type=MESH)

    for stage in range(4):
        for j in (1, 2, 3):
            share(stage, j).start()
        for j in (1, 2, 3):
            share(stage, j).wait_recv()
        high = joint[stage, 0]
        for j in range(3):
            high = jnp.maximum(high, shared[stage, j, 0])
        heaps = [joint[stage, 1] * jnp.exp(joint[stage, 0] - high)]
        for j in range(3):
            heaps.append(shared[stage, j, 1] * jnp.exp(shared[stage, j, 0] - high))
        heap = (heaps[0] + heaps[2]) + (heaps[1] + heaps[3])
        if stage < 3:
            joint[stage + 1, 0] = high
            joint[stage + 1, 1] = heap
    log_all = high + jnp.log(heap)
    joint[4, 0] = log_all
    home_row = joint[4, 0, pl.ds(lax.div(h, 2), 1), :]
    log_ref[...] = jnp.where(lax.rem(h, 2) == 0, home_row[:, 0:PART], home_row[:, PART:2 * PART])
    groups = []
    for q in range(4):
        pair = jnp.concatenate([log_all[2 * q:2 * q + 1, :], log_all[2 * q + 1:2 * q + 2, :]], axis=1)
        rows = jnp.concatenate(split(pair) + [jnp.zeros((5, 256), F32)], axis=0).astype(BF16)
        back_row = nt_dot(rows, maps[q])
        groups.append(back_row[0:1, :] + back_row[1:2, :] + back_row[2:3, :])
    slot_log = jnp.concatenate(groups, axis=1)
    scale = float(N_CLS * PRUNE * ORI_DEV)
    level = jnp.where(row < 0.0, 0.0, scale * jnp.exp(peak - slot_log))
    for d in range(TRANS):
        rows = pl.ds(d * ORI_DEV, ORI_DEV)
        w_ref[rows, :] = (s_ref[rows, :] * level).astype(BF16)
    grouped = nt_dot((mass * level).astype(BF16), slot_pick)
    high = grouped.astype(BF16)
    t_ref[:, 0:GROUPS] = high
    t_ref[:, GROUPS:2 * GROUPS] = (grouped - high.astype(F32)).astype(BF16)

    def drain(step, carry):
        peer = wrap(h + step, N_ORI)
        parcel(peer, step).wait_send()
        note(peer, step).wait_send()
        return carry

    lax.fori_loop(1, N_ORI, drain, 0)

    def drain_blocks(slot, carry):
        full_copy(0, c, c, slot).wait_send()
        piece_copy(0, c, 0, c, slot).wait_send()
        return carry

    lax.fori_loop(0, 20, drain_blocks, 0)
    for stage in range(4):
        for j in (1, 2, 3):
            share(stage, j).wait_send()
    save.wait()


def expect(images, projections, ctf_table, index_row, centre, ranges, inv_row, cosine, sine):
    vmem = pl.BlockSpec(memory_space=pltpu.VMEM)
    hbm = pl.BlockSpec(memory_space=pl.ANY)
    rows = TRANS * ORI_DEV
    dma = pltpu.SemaphoreType.DMA
    return pl.pallas_call(
        expect_kernel,
        out_shape=(
            jax.ShapeDtypeStruct((SLOTS, 2 * COEFS), BF16),
            jax.ShapeDtypeStruct((rows, SLOTS), BF16),
            jax.ShapeDtypeStruct((ORI_DEV, 2 * GROUPS), BF16),
            jax.ShapeDtypeStruct((GROUPS, COEFS), BF16),
            jax.ShapeDtypeStruct((1, PART), F32),
        ),
        in_specs=[hbm, hbm] + [vmem] * 7,
        out_specs=(hbm, vmem, vmem, vmem, vmem),
        scratch_shapes=[
            pltpu.VMEM((PART, 2, CHUNK), BF16),
            pltpu.VMEM((ORI_DEV, 2, COEFS), BF16),
            pltpu.VMEM((N_ORI, CAP, 2 * CHUNK), BF16),
            pltpu.VMEM((N_ORI, 4, 128), F32),
            pltpu.VMEM((N_ORI, 4, 128), F32),
            pltpu.VMEM((SLOTS, 2 * COEFS), BF16),
            pltpu.VMEM((N_CLS, rows, 4 * CHUNK), BF16),
            pltpu.VMEM((rows, SLOTS), F32),
            pltpu.VMEM((5, 2, N_ORI // 2, 128), F32),
            pltpu.VMEM((4, 3, 2, N_ORI // 2, 128), F32),
            pltpu.VMEM((4, 128, 256), BF16),
            pltpu.VMEM((SLOTS, 2 * COEFS), BF16),
            pltpu.VMEM((SLOTS, 256), BF16),
            pltpu.VMEM((N_CLS, 256, 3 * CHUNK), BF16),
            pltpu.VMEM((HALF, 4 * CHUNK), BF16),
            pltpu.VMEM((HALF, 4 * CHUNK), BF16),
            dma((4,)),
            dma((N_ORI,)),
            dma((N_ORI,)),
            dma((N_ORI,)),
            dma((N_ORI,)),
            dma((20,)),
            dma((20,)),
            dma((2, N_CLS, 2)),
            dma((4, 4)),
            dma((4, 4)),
        ],
        compiler_params=pltpu.CompilerParams(
            collective_id=0, has_side_effects=True, vmem_limit_bytes=VMEM_LIMIT
        ),
        name="expect",
    )(images, projections, ctf_table, index_row, centre, ranges, inv_row, cosine, sine)


WIDE = 4


def back_kernel(w_ref, t_ref, y_ref, cw_ref, cos_ref, sin_ref, data_ref, ctf_ref, d_ref):
    cw = cw_ref[...]
    ctf_ref[0] = jnp.dot(t_ref[...], jnp.concatenate([cw, cw], axis=0), preferred_element_type=F32)
    d_ref[...] = jnp.dot(w_ref[...], y_ref[...], preferred_element_type=F32)

    def turn(minus, zero, plus, cd, sd):
        real = zero[0] + cd * (plus[0] + minus[0]) + sd * (plus[1] - minus[1])
        imag = zero[1] + cd * (plus[1] + minus[1]) - sd * (plus[0] - minus[0])
        return real, imag

    for part in range(WIDE):
        base = part * 2 * CHUNK
        cols = slice(part * CHUNK, part * CHUNK + CHUNK)
        for block in range(ORI_DEV // 16):
            outer = []
            for dx in range(3):
                inner = []
                for dy in range(3):
                    rows = pl.ds((dx * 3 + dy) * ORI_DEV + block * 16, 16)
                    inner.append((d_ref[rows, base:base + CHUNK], d_ref[rows, base + CHUNK:base + 2 * CHUNK]))
                outer.append(turn(*inner, cos_ref[5:6, cols], sin_ref[5:6, cols]))
            real, imag = turn(*outer, cos_ref[7:8, cols], sin_ref[7:8, cols])
            data_ref[0, block * 16:(block + 1) * 16, 0, cols] = real
            data_ref[0, block * 16:(block + 1) * 16, 1, cols] = imag


def back(w, t, ys, cw, cosine, sine):
    full = lambda *shape: pl.BlockSpec(shape, lambda j: (0,) * len(shape))
    return pl.pallas_call(
        back_kernel,
        out_shape=(
            jax.ShapeDtypeStruct((1, ORI_DEV, 2, COEFS), F32),
            jax.ShapeDtypeStruct((1, ORI_DEV, COEFS), F32),
        ),
        grid=(N_CLS // WIDE,),
        in_specs=[
            full(TRANS * ORI_DEV, SLOTS),
            full(ORI_DEV, 2 * GROUPS),
            pl.BlockSpec((SLOTS, WIDE * 2 * CHUNK), lambda j: (0, j)),
            pl.BlockSpec((GROUPS, WIDE * CHUNK), lambda j: (0, j)),
            pl.BlockSpec((16, WIDE * CHUNK), lambda j: (0, j)),
            pl.BlockSpec((16, WIDE * CHUNK), lambda j: (0, j)),
        ],
        out_specs=(
            pl.BlockSpec((1, ORI_DEV, 2, WIDE * CHUNK), lambda j: (0, 0, 0, j)),
            pl.BlockSpec((1, ORI_DEV, WIDE * CHUNK), lambda j: (0, 0, j)),
        ),
        scratch_shapes=[pltpu.VMEM((TRANS * ORI_DEV, WIDE * 2 * CHUNK), F32)],
        compiler_params=pltpu.CompilerParams(vmem_limit_bytes=VMEM_LIMIT),
        name="back",
    )(w, t, ys, cw, cosine, sine)


def shards(images, projections, ctf_table, ctf_index, centre, ranges, inv_noise):
    cosine, sine = (jnp.asarray(table) for table in step_tables())
    ys, w, t, cw, log_row = expect(
        images, projections, ctf_table, ctf_index.reshape(1, PART), centre.T, ranges.T,
        inv_noise.reshape(1, COEFS), cosine, sine,
    )
    data, ctf = back(w, t, ys, cw, cosine, sine)
    return data, ctf, log_row.reshape(PART)


def solution(mesh):
    placed = (
        P("ori", None, None),
        P("cls", "ori", None, None),
        P(),
        P("ori"),
        P("ori", None),
        P("ori", None),
        P(),
    )
    return jax.shard_map(
        shards,
        mesh=mesh,
        in_specs=placed,
        out_specs=(P("cls", "ori", None, None), P("cls", "ori", None), P("ori")),
        check_vma=False,
    )
```

time: 990 us -> 86.3 us (0.09); the launches traced: 976 us -> 86.2 us
  other arithmetic: 472 us -> 0 us
  local copies, waits for them, and re-layouts: 235 us -> 0.52 us
  waiting for transfers between devices: 93.2 us -> 0 us
  Pallas kernels: 0 us -> 85 us
  matrix products: 64.4 us -> 0 us
  starting transfers between devices: 41.1 us -> 0 us
  blocking collectives: 35.6 us -> 0 us
  loops' own time: 32.9 us -> 0 us
    another operation x26 -> x0, other arithmetic: 327 us -> none
    all_to_all x5 -> x0, waiting for transfers between devices: 93.2 us -> none  [the longest x1 81.5 us: shards(): lax.all_to_all(parcel.reshape(ori_count, capacity, 2, coef_count), 'ori',...]
    pallas_call x0 -> x2, Pallas kernels: none -> 85 us  [the longest x1 75.7 us: expect(): pl.pallas_call(expect_kernel, out_shape=(jax.ShapeDtypeStruct((SLOTS, 2 *...]
    another operation x15 -> x0, local copies, waits for them, and re-layouts: 75 us -> none  [the longest x8 74.5 us: rotate_block(): rotated = jnp.stack([real_part, imag_part], axis=2).astype(jnp.bfloat16)]
    while x25 -> x0, local copies, waits for them, and re-layouts: 68.8 us -> none
    dot_general x26 -> x0, matrix products: 64.4 us -> none  [the longest x8 29.1 us: accumulate(): lax.dot_general(rounded, rotated, (((0,), (0,)), ((), ())), preferred_ele...]
    gather x14 -> x0, local copies, waits for them, and re-layouts: 48.6 us -> none  [the longest x2 24.6 us: shards(): parcel = images[source] * filled[:, None, None].astype(jnp.bfloat16)]
    all_to_all x5 -> x0, starting transfers between devices: 41.1 us -> none  [the longest x1 16.2 us: shards(): lax.all_to_all(mass_classes.reshape(ori_count, capacity), 'ori', split_ax...]
  transfers between devices with their start and end apart: 5 -> 0, of which waited for: 4 -> 0; matrix products, arithmetic and copies ran while one was open for 5% -> 0% of each run, Pallas kernels for 0% -> 0%
where the time goes in v1:
time: 86.3 us; the launch traced here: 86.2 us
  Pallas kernels  85 us (98%)
    pallas_call x1, Pallas kernels, expect(): pl.pallas_call(expect_kernel, out_shape=(jax.ShapeDtypeStruct((SLOTS, 2 *...  75.7 us
    pallas_call x1, Pallas kernels, back(): pl.pallas_call(back_kernel, out_shape=(jax.ShapeDtypeStruct((1, ORI_DEV,...  9.33 us

profile of v1, /device:TPU:1, one launch (start us, length us, event | category | flops | bytes accessed | tf_op | source)
XLA Modules:
  0.0 86.2 jit_solution(17218463008091107588)
XLA Ops:
  0.6 75.7 %expect.1 = (bf16[512,4096]{1,0:T(8,128)(2,1)}, bf16[1152,512]{1,0:T(8,128)(2,1)}, bf16[128,128]{1,0:T(8,128)(2,1)}, bf16[64,2048]{1,0:T(8,128)(2,1)}, f32[1,64]{1,0:T(1,128)}) custom-call(bf16[64,2,2048]{2,1,0:T(2,128)(2,1)} %images_ref.1, bf16[1,128,2,2048]{3,2,1,0:T(2,128)(2,1)} %proj_ref.1, bf16[64,2048]{1,0:T(8,128)(2,1)} %ctf_ref.1, s32[1,64]{1,0:T(1,128)} %bitcast.8, ...), custom_call_target="tpu_custom_call" | custom-call | tf_op jit(solution)/shard_map/expect/pallas_call | solution.py:459
  76.3 0.0 copy-start
  76.3 9.3 %back.1 = (f32[1,128,2,2048]{3,2,1,0:T(2,128)}, f32[1,128,2048]{2,1,0:T(8,128)}) custom-call(bf16[1152,512]{1,0:T(8,128)(2,1)} %get-tuple-element.10.w_ref, bf16[128,128]{1,0:T(8,128)(2,1)} %get-tuple-element.11.t_ref, bf16[512,4096]{1,0:T(8,128)(2,1)} %get-tuple-element.12.y_ref, bf16[64,2048]{1,0:T(8,128)(2,1)} %get-tuple-element.13.cw_ref, ...), custom_call_target="tpu_custom_call" | custom-call | tf_op jit(solution)/shard_map/back/pallas_call | solution.py:536
  85.7 0.0 copy-done
  85.7 0.5 copy.13
Async XLA Ops:
  76.3 9.3 %copy-start = (f32[1,64]{1,0:T(1,128)S(1)}, f32[1,64]{1,0:T(1,128)}, u32[]{:S(2)}) copy-start(f32[1,64]{1,0:T(1,128)} %get-tuple-element.16) | copy-start | bytes 772

commit v2 on v1

--- a/solution.py
+++ b/solution.py
@@ -3,6 +3,7 @@
 
 import jax
 import jax.numpy as jnp
+import ml_dtypes
 import numpy as np
 from jax import lax
 from jax.experimental import pallas as pl
@@ -70,10 +71,25 @@
 
 HALF = SLOTS // 2
 COMBOS = 96
+EARLY = 11
 PIECE = HALF // 2
 
 
-def expect_kernel(images_ref, proj_ref, ctf_ref, index_ref, centre_ref, ranges_ref, inv_ref, cos_ref, sin_ref,
+def wave_table():
+    k = np.arange(COEFS)
+    which = np.arange(COMBOS)[:, None]
+    turn = ((k % KX) * (which // 9 - 4) + (k // KX - KY // 2) * (which % 9 - 4)) * RADIANS
+    table = np.zeros((N_CLS, 2 * COMBOS, 2 * CHUNK), ml_dtypes.bfloat16)
+    for n, wave in enumerate((np.cos(turn), np.sin(turn))):
+        coarse = wave.astype(ml_dtypes.bfloat16)
+        fine = (wave - coarse.astype(np.float64)).astype(ml_dtypes.bfloat16)
+        for half, value in enumerate((coarse, fine)):
+            cut = value.reshape(COMBOS, N_CLS, CHUNK).transpose(1, 0, 2)
+            table[:, half * COMBOS:(half + 1) * COMBOS, n * CHUNK:(n + 1) * CHUNK] = cut
+    return table
+
+
+def expect_kernel(images_ref, proj_ref, wave_ref, ctf_ref, index_ref, centre_ref, ranges_ref, inv_ref, cos_ref, sin_ref,
                   yout_ref, w_ref, t_ref, cw_ref, log_ref,
                   ximg, pbuf, send, meta, metain, ys, pd, s_ref, joint, shared, maps, yc, hot, trig, buf_a, buf_b,
                   local_sem, z_send, z_recv, m_send, m_recv, f_send, p_send, g_recv, e_send, e_recv):
@@ -114,6 +130,10 @@
     get_image.start()
     get_proj = pltpu.make_async_copy(proj_ref.at[0], pbuf, local_sem.at[1])
     get_proj.start()
+    get_wave = pltpu.make_async_copy(
+        wave_ref, trig.at[:, pl.ds(GROUPS, 2 * COMBOS), pl.ds(0, 2 * CHUNK)], local_sem.at[4]
+    )
+    get_wave.start()
 
     index_row = index_ref[...].astype(F32)
     member_t = jnp.zeros((N_ORI, PART), F32)
@@ -176,6 +196,7 @@
     metain[h] = meta[h]
 
     get_proj.wait()
+    get_wave.wait()
     s_ref[0:ORI_DEV, 0:GROUPS] = jnp.zeros((ORI_DEV, GROUPS), F32)
 
     def turn_chunk(j, carry):
@@ -197,22 +218,12 @@
                 coarse = turned[n].astype(BF16)
                 pd[j, rows, n * CHUNK:(n + 1) * CHUNK] = coarse
                 pd[j, rows, (2 + n) * CHUNK:(3 + n) * CHUNK] = (turned[n] - coarse.astype(F32)).astype(BF16)
-        k = j * CHUNK + iota((1, CHUNK), 1)
-        kx = lax.rem(k, KX)
-        ky = lax.div(k, KX) - KY // 2
-        which = iota((COMBOS, 1), 0)
-        angles = (kx * (lax.div(which, 9) - 4) + ky * (lax.rem(which, 9) - 4)).astype(F32) * RADIANS
-        for n, wave in ((0, jnp.cos(angles)), (1, jnp.sin(angles))):
-            coarse = wave.astype(BF16)
-            span = slice(n * CHUNK, (n + 1) * CHUNK)
-            trig[j, 0:GROUPS, span] = jnp.zeros((GROUPS, CHUNK), BF16)
-            trig[j, GROUPS:GROUPS + COMBOS, span] = coarse
-            trig[j, GROUPS + COMBOS:256, span] = (wave - coarse.astype(F32)).astype(BF16)
+        trig[j, 0:GROUPS, 0:2 * CHUNK] = jnp.zeros((GROUPS, 2 * CHUNK), BF16)
         trig[j, 0:GROUPS, 2 * CHUNK:3 * CHUNK] = ctf_ref[:, cols]
         trig[j, GROUPS:256, 2 * CHUNK:3 * CHUNK] = jnp.zeros((2 * COMBOS, CHUNK), BF16)
         return carry
 
-    lax.fori_loop(0, N_CLS, turn_chunk, 0)
+    lax.fori_loop(0, EARLY, turn_chunk, 0)
 
     def arrive(step, carry):
         peer = wrap(h - step, N_ORI)
@@ -254,6 +265,7 @@
     for half in (0, 1):
         second_sends(half, 0, 0)
 
+    lax.fori_loop(EARLY, N_CLS, turn_chunk, 0)
     row = slot_row(metain, 0) - 1.0
     slot_pick = (iota((GROUPS, SLOTS), 0).astype(F32) == row).astype(BF16)
     combo_pick = (iota((COMBOS, SLOTS), 0).astype(F32) == slot_row(metain, 2)).astype(BF16)
@@ -451,7 +463,7 @@
     save.wait()
 
 
-def expect(images, projections, ctf_table, index_row, centre, ranges, inv_row, cosine, sine):
+def expect(images, projections, waves, ctf_table, index_row, centre, ranges, inv_row, cosine, sine):
     vmem = pl.BlockSpec(memory_space=pltpu.VMEM)
     hbm = pl.BlockSpec(memory_space=pl.ANY)
     rows = TRANS * ORI_DEV
@@ -465,7 +477,7 @@
             jax.ShapeDtypeStruct((GROUPS, COEFS), BF16),
             jax.ShapeDtypeStruct((1, PART), F32),
         ),
-        in_specs=[hbm, hbm] + [vmem] * 7,
+        in_specs=[hbm, hbm, hbm] + [vmem] * 7,
         out_specs=(hbm, vmem, vmem, vmem, vmem),
         scratch_shapes=[
             pltpu.VMEM((PART, 2, CHUNK), BF16),
@@ -484,7 +496,7 @@
             pltpu.VMEM((N_CLS, 256, 3 * CHUNK), BF16),
             pltpu.VMEM((HALF, 4 * CHUNK), BF16),
             pltpu.VMEM((HALF, 4 * CHUNK), BF16),
-            dma((4,)),
+            dma((5,)),
             dma((N_ORI,)),
             dma((N_ORI,)),
             dma((N_ORI,)),
@@ -499,7 +511,7 @@
             collective_id=0, has_side_effects=True, vmem_limit_bytes=VMEM_LIMIT
         ),
         name="expect",
-    )(images, projections, ctf_table, index_row, centre, ranges, inv_row, cosine, sine)
+    )(images, projections, waves, ctf_table, index_row, centre, ranges, inv_row, cosine, sine)
 
 
 WIDE = 4
@@ -561,7 +573,7 @@
 def shards(images, projections, ctf_table, ctf_index, centre, ranges, inv_noise):
     cosine, sine = (jnp.asarray(table) for table in step_tables())
     ys, w, t, cw, log_row = expect(
-        images, projections, ctf_table, ctf_index.reshape(1, PART), centre.T, ranges.T,
+        images, projections, jnp.asarray(wave_table()), ctf_table, ctf_index.reshape(1, PART), centre.T, ranges.T,
         inv_noise.reshape(1, COEFS), cosine, sine,
     )
     data, ctf = back(w, t, ys, cw, cosine, sine)

time: 86.3 us -> 80.9 us (0.937)
  Pallas kernels: 85 us -> 79.6 us
    pallas_call x1, Pallas kernels: 75.7 us -> 70.3 us  [expect(): pl.pallas_call(expect_kernel, out_shape=(jax.ShapeDtypeStruct((SLOTS, 2 *...]
where the time goes in v2:
time: 80.9 us; the launch traced here: 80.8 us
  Pallas kernels  79.6 us (98%)
    pallas_call x1, Pallas kernels, expect(): pl.pallas_call(expect_kernel, out_shape=(jax.ShapeDtypeStruct((SLOTS, 2 *...  70.3 us
    pallas_call x1, Pallas kernels, back(): pl.pallas_call(back_kernel, out_shape=(jax.ShapeDtypeStruct((1, ORI_DEV,...  9.33 us

profile of v2, /device:TPU:1, one launch (start us, length us, event | category | flops | bytes accessed | tf_op | source)
XLA Modules:
  0.0 80.8 jit_solution(1213164947533744912)
XLA Ops:
  0.6 70.3 %expect.1 = (bf16[512,4096]{1,0:T(8,128)(2,1)}, bf16[1152,512]{1,0:T(8,128)(2,1)}, bf16[128,128]{1,0:T(8,128)(2,1)}, bf16[64,2048]{1,0:T(8,128)(2,1)}, f32[1,64]{1,0:T(1,128)}) custom-call(bf16[64,2,2048]{2,1,0:T(2,128)(2,1)} %images_ref.1, bf16[1,128,2,2048]{3,2,1,0:T(2,128)(2,1)} %proj_ref.1, bf16[16,192,256]{2,1,0:T(8,128)(2,1)} %constant.8.clone.wave_ref, ...), custom_call_target="tpu_custom_call" | custom-call | tf_op jit(solution)/shard_map/expect/pallas_call | solution.py:471
  70.9 0.0 copy-start
  70.9 9.3 %back.1 = (f32[1,128,2,2048]{3,2,1,0:T(2,128)}, f32[1,128,2048]{2,1,0:T(8,128)}) custom-call(bf16[1152,512]{1,0:T(8,128)(2,1)} %get-tuple-element.10.w_ref, bf16[128,128]{1,0:T(8,128)(2,1)} %get-tuple-element.11.t_ref, bf16[512,4096]{1,0:T(8,128)(2,1)} %get-tuple-element.12.y_ref, bf16[64,2048]{1,0:T(8,128)(2,1)} %get-tuple-element.13.cw_ref, ...), custom_call_target="tpu_custom_call" | custom-call | tf_op jit(solution)/shard_map/back/pallas_call | solution.py:548
  80.3 0.0 copy-done
  80.3 0.5 copy.14
Async XLA Ops:
  70.9 9.3 %copy-start = (f32[1,64]{1,0:T(1,128)S(1)}, f32[1,64]{1,0:T(1,128)}, u32[]{:S(2)}) copy-start(f32[1,64]{1,0:T(1,128)} %get-tuple-element.16) | copy-start | bytes 772
